TPU v7x, 128 devices: a whole 4x4x4 slice. The times are simulated.
128 devices in a mesh: section: 2 (over x_lo), dp: 16 (over x_hi, y, core), mp: 4 (over z).
Axes of the slice: x: 4 (x_hi: 2, x_lo: 2; x = x_hi * 2 + x_lo), y: 4, z: 4, core: 2. Of those that a mesh axis runs over, the one named last changes fastest.
Arguments:
- hidden: bfloat16 [2, 16, 256, 5120], P('section', 'dp'), may hold values from -6 to 6
- gain: float32 [2, 5120], P('section'), may hold values from 0.5 to 2
- w_first: bfloat16 [2, 5120, 2560], P('section', 'dp', 'mp'), may hold values from -0.078125 to 0.078125
- w_second: bfloat16 [2, 5120, 2560], P('section', 'dp', 'mp'), may hold values from -0.078125 to 0.078125
- lengths: int32 [16, 2], P('dp'), may hold values from 32 to 256, as said below
- cotangent: bfloat16 [2, 16, 256, 5120], P('section', 'dp'), may hold values from -6 to 6
Outputs:
- result: bfloat16 [2, 16, 256, 5120], P('section', 'dp')
- d_hidden: bfloat16 [2, 16, 256, 5120], P('section', 'dp')
- d_gain: float32 [2, 5120], P('section', 'dp')
- d_first: float32 [2, 5120, 2560], P('section', 'dp', 'mp')
- d_second: float32 [2, 5120, 2560], P('section', 'dp', 'mp')
Inputs may be any that keep to these rules, and one draw needn't show every extreme that they name: `lengths`: each row's source count and target count; positions at or past a count are padding.
All inputs are finite; a program needn't handle non-finite values.
Results may differ from a plain program's by a relative error of at most 0.017.
Values may be sent and summed in bfloat16 or wider, within the bound.
A program may use at most 128 MiB of HBM per device.

v0:
```python
import math
import jax
import jax.numpy as jnp
from jax import lax
from jax.sharding import PartitionSpec as P

HEAD = 128
EPS = 1e-06
MASKED = -1e30


def passed_along(shard, axis, by):
    peers = lax.axis_size(axis)
    pairs = [(i, i + by) for i in range(peers) if 0 <= i + by < peers]
    return lax.ppermute(shard, axis, pairs)


def contract_rows(left, right):
    return lax.dot_general(
        left, right, (((0,), (0,)), ((), ())), preferred_element_type=jnp.float32
    )


def contract_last(left, right):
    return lax.dot_general(
        left, right, (((1,), (1,)), ((), ())), preferred_element_type=jnp.float32
    )


def total_features(partial_value):
    return lax.psum(partial_value, "mp")


def split_heads(values_in):
    batch_size, length, columns = values_in.shape
    return values_in.reshape(batch_size, length, columns // HEAD, HEAD)


def attend(queries, keys, values, key_count):
    batch_size, length, columns = queries.shape
    scale = 1.0 / math.sqrt(HEAD)
    scores = (
        jnp.einsum(
            "bqhd,bkhd->bhqk",
            split_heads(queries),
            split_heads(keys),
            preferred_element_type=jnp.float32,
        )
        * scale
    )
    visible = jnp.arange(length)[None, None, None, :] < key_count[:, None, None, None]
    scores = jnp.where(visible, scores, MASKED)
    weights = jax.nn.softmax(scores, axis=-1)
    weights_low = weights.astype(jnp.bfloat16)
    context = jnp.einsum(
        "bhqk,bkhd->bqhd", weights_low, split_heads(values), preferred_element_type=jnp.float32
    )
    return (context.reshape(batch_size, length, columns).astype(jnp.bfloat16), weights, weights_low)


def attend_back(grad_context, queries, keys, values, weights, weights_low):
    batch_size, length, columns = queries.shape
    scale = 1.0 / math.sqrt(HEAD)
    grad_heads = split_heads(grad_context)
    grad_weights = jnp.einsum(
        "bqhd,bkhd->bhqk", grad_heads, split_heads(values), preferred_element_type=jnp.float32
    )
    grad_values = jnp.einsum(
        "bhqk,bqhd->bkhd", weights_low, grad_heads, preferred_element_type=jnp.float32
    )
    centered = grad_weights - jnp.sum(weights * grad_weights, axis=-1, keepdims=True)
    grad_scores = (weights * centered * scale).astype(jnp.bfloat16)
    grad_queries = jnp.einsum(
        "bhqk,bkhd->bqhd", grad_scores, split_heads(keys), preferred_element_type=jnp.float32
    )
    grad_keys = jnp.einsum(
        "bhqk,bqhd->bkhd", grad_scores, split_heads(queries), preferred_element_type=jnp.float32
    )
    shape_out = (batch_size, length, columns)
    return (
        grad_queries.reshape(shape_out).astype(jnp.bfloat16),
        grad_keys.reshape(shape_out).astype(jnp.bfloat16),
        grad_values.reshape(shape_out).astype(jnp.bfloat16),
    )


def shards(hidden, gain, w_first, w_second, lengths, cotangent):
    encoder = lax.axis_index("section") == 0
    states = hidden[0]
    batch_size, length, width = states.shape
    total_rows = batch_size * length
    gains = gain[0]
    wide = states.astype(jnp.float32)
    inverse = lax.rsqrt(jnp.mean(wide * wide, axis=-1, keepdims=True) + EPS)
    unit = wide * inverse
    normed = (unit * gains).astype(jnp.bfloat16)
    normed_rows = normed.reshape(total_rows, width)
    full_first, full_second = (
        lax.all_gather(w_first[0], "dp", axis=0, tiled=True),
        lax.all_gather(w_second[0], "dp", axis=0, tiled=True),
    )
    columns = full_first.shape[1]
    proj_shape = (batch_size, length, columns)
    first_proj = (
        jnp.dot(normed_rows, full_first, preferred_element_type=jnp.float32)
        .astype(jnp.bfloat16)
        .reshape(proj_shape)
    )

    def values_encoder(operand):
        return (
            jnp.dot(normed_rows, full_second, preferred_element_type=jnp.float32)
            .astype(jnp.bfloat16)
            .reshape(proj_shape)
        )

    def values_decoder(operand):
        return jnp.zeros(proj_shape, jnp.bfloat16)

    second_proj = lax.cond(encoder, values_encoder, values_decoder, 0)
    keys, values = passed_along((first_proj, second_proj), "section", 1)
    heads_here = columns // HEAD
    weight_shape = (batch_size, heads_here, length, length)

    def forward_decoder(operand):
        context, weights, weights_low = attend(first_proj, keys, values, lengths[:, 0])
        out_part = contract_last(context.reshape(total_rows, columns), full_second)
        return (context, weights, weights_low, out_part)

    def forward_encoder(operand):
        return (
            jnp.zeros(proj_shape, jnp.bfloat16),
            jnp.zeros(weight_shape, jnp.float32),
            jnp.zeros(weight_shape, jnp.bfloat16),
            jnp.zeros((total_rows, width), jnp.float32),
        )

    context, weights, weights_low, out_part = lax.cond(encoder, forward_encoder, forward_decoder, 0)
    wide_rows = wide.reshape(total_rows, width)
    unit_rows = unit.reshape(total_rows, width)
    inverse_rows = inverse.reshape(total_rows, 1)
    output_rows = (wide_rows + total_features(out_part)).astype(jnp.bfloat16)
    result = jnp.where(encoder, normed, output_rows.reshape(batch_size, length, width))
    target_keep = jnp.arange(length)[None, :] < lengths[:, 1][:, None]
    grad_out = jnp.where(target_keep[:, :, None], cotangent[0], jnp.zeros((), jnp.bfloat16))
    grad_out_rows = grad_out.reshape(total_rows, width)

    def backward_decoder(operand):
        grad_context = (
            jnp.dot(grad_out_rows, full_second, preferred_element_type=jnp.float32)
            .astype(jnp.bfloat16)
            .reshape(proj_shape)
        )
        return attend_back(grad_context, first_proj, keys, values, weights, weights_low)

    def backward_encoder(operand):
        empty = jnp.zeros(proj_shape, jnp.bfloat16)
        return (empty, empty, empty)

    grad_query, grad_key, grad_value = lax.cond(encoder, backward_encoder, backward_decoder, 0)
    back_key, back_value = passed_along((grad_key, grad_value), "section", -1)
    grad_first = jnp.where(encoder, back_key, grad_query).reshape(total_rows, columns)
    grad_second = jnp.where(encoder, back_value, jnp.zeros((), jnp.bfloat16)).reshape(
        total_rows, columns
    )
    second_left = jnp.where(encoder, normed, grad_out).reshape(total_rows, width)
    second_right = jnp.where(encoder, back_value, context).reshape(total_rows, columns)
    weight_first = contract_rows(normed_rows, grad_first)
    weight_second = contract_rows(second_left, second_right)

    def back_encoder(operand):
        return contract_last(grad_first, full_first) + contract_last(grad_second, full_second)

    def back_decoder(operand):
        return contract_last(grad_first, full_first)

    back_part = lax.cond(encoder, back_encoder, back_decoder, 0)
    extra_rows = jnp.where(encoder, cotangent[0].astype(jnp.float32), 0.0).reshape(
        total_rows, width
    )
    residual_rows = jnp.where(encoder, 0.0, grad_out.astype(jnp.float32)).reshape(total_rows, width)
    grad_normed = total_features(back_part) + extra_rows
    scaled = grad_normed * gains
    inner = jnp.mean(scaled * unit_rows, axis=-1, keepdims=True)
    grad_states = (inverse_rows * (scaled - unit_rows * inner) + residual_rows).astype(jnp.bfloat16)
    gain_part = jnp.sum(grad_normed * unit_rows, axis=0)
    first_sum, second_sum, gain_sum = (
        lax.psum_scatter(
            weight_first.astype(jnp.bfloat16), "dp", scatter_dimension=0, tiled=True
        ).astype(jnp.float32),
        lax.psum_scatter(
            weight_second.astype(jnp.bfloat16), "dp", scatter_dimension=0, tiled=True
        ).astype(jnp.float32),
        lax.psum_scatter(
            gain_part.astype(jnp.bfloat16), "dp", scatter_dimension=0, tiled=True
        ).astype(jnp.float32),
    )
    return (
        result[None],
        grad_states.reshape(batch_size, length, width)[None],
        gain_sum[None],
        first_sum[None],
        second_sum[None],
    )


def solution(mesh):
    return jax.shard_map(
        shards,
        mesh=mesh,
        in_specs=(
            P("section", "dp", None, None),
            P("section", None),
            P("section", "dp", "mp"),
            P("section", "dp", "mp"),
            P("dp", None),
            P("section", "dp", None, None),
        ),
        out_specs=(
            P("section", "dp", None, None),
            P("section", "dp", None, None),
            P("section", "dp"),
            P("section", "dp", "mp"),
            P("section", "dp", "mp"),
        ),
        check_vma=False,
    )
```

profile of v0, /device:TPU:0, one launch (start us, length us, event | category | flops | bytes accessed | tf_op | source)
XLA Modules:
  0.0 682.9 jit_solution(3879700864426107040)
XLA Ops:
  7.2 0.0 copy-start
  7.2 0.0 copy-start.10
  7.2 0.0 all-gather.5.cloned.1.call-start
  7.2 0.7 all-gather.5.cloned.1.call-update
  7.9 0.0 all-gather.7.cloned.1.call-start
  8.0 0.7 all-gather.7.cloned.1.call-update
  8.7 0.0 reduce-scatter.3.cloned.1.call-start
  8.7 1.2 slice.6
  10.0 0.6 iota_compare_fusion.1
  10.6 2.3 fusion.36
  13.0 0.0 copy-done
  13.0 3.0 fusion.28
  16.0 62.1 %all-gather.5.cloned.1.call-done = bf16[1,5120,640]{2,1,0:T(8,128)(2,1)} async-done(((bf16[1,320,640]{2,1,0:T(8,128)(2,1)}), bf16[1,5120,640]{2,1,0:T(8,128)(2,1)}) %all-gather.5.cloned.1.call-update) | async-done | bytes 6553616 | tf_op jit(solution)/shard_map/all_gather | solution.py:99
  78.1 0.0 copy-done.10
  78.1 5.1 convolution_convert_fusion.8
  83.2 3.2 collective-permute-start
  86.4 59.0 %all-gather.7.cloned.1.call-done = bf16[1,5120,640]{2,1,0:T(8,128)(2,1)} async-done(((bf16[1,320,640]{2,1,0:T(8,128)(2,1)}), bf16[1,5120,640]{2,1,0:T(8,128)(2,1)}) %all-gather.7.cloned.1.call-update) | async-done | bytes 6553616 | tf_op jit(solution)/shard_map/all_gather | solution.py:100
  145.4 5.9 conditional.4
  145.4 5.9 fusion
  151.3 0.0 copy-start.11
  151.3 0.9 copy.53
  152.2 2.0 collective-permute-start.1
  154.2 3.5 bitcast_select_fusion
  157.7 0.0 collective-permute-done
  157.7 3.8 collective-permute-done.1
  161.5 0.0 copy-done.9
  161.5 4.9 conditional.5
  161.5 1.2 broadcast.147
  162.7 2.9 broadcast.149
  165.6 0.8 broadcast.146.clone
  166.3 1.5 conditional.6
  166.3 0.8 broadcast.151
  167.1 0.8 broadcast.151.clone.1
  167.9 1.2 copy.59
  169.1 1.3 collective-permute-start.2
  170.4 40.9 %collective-permute-done.2 = bf16[1,256,640]{2,1,0:T(8,128)(2,1)S(1)} collective-permute-done((bf16[1,256,640]{2,1,0:T(8,128)(2,1)S(1)}, bf16[1,256,640]{2,1,0:T(8,128)(2,1)S(1)}, u32[]{:S(2)}, u32[]{:S(2)}) %collective-permute-start.2) | collective-permute-done | bytes 327712 | tf_op jit(solution)/shard_map/ppermute | solution.py:15
  211.3 5.1 convolution_convert_fusion.7
  216.4 0.0 reduce-scatter.3.cloned.1.call-update
  216.5 0.0 reduce-scatter.5.cloned.1.call-start
  216.5 0.9 copy-done.8
  217.4 0.9 copy.61
  218.3 1.3 collective-permute-start.3
  219.6 9.6 %collective-permute-done.3 = bf16[1,256,640]{2,1,0:T(8,128)(2,1)S(1)} collective-permute-done((bf16[1,256,640]{2,1,0:T(8,128)(2,1)}, bf16[1,256,640]{2,1,0:T(8,128)(2,1)S(1)}, u32[]{:S(2)}, u32[]{:S(2)}) %collective-permute-start.3) | collective-permute-done | bytes 327712 | tf_op jit(solution)/shard_map/ppermute | solution.py:15
  229.2 7.8 %convolution_convert_fusion.6 = bf16[5120,640]{1,0:T(8,128)(2,1)} fusion(bf16[1,1,256,5120]{3,2,1,0:T(8,128)(2,1)} %param.19, pred[256]{0:T(512)(128)(4,1)S(1)} %iota_compare_fusion.1, pred[]{:T(512)} %eq.3, bf16[1,1,256,5120]{3,2,1,0:T(8,128)(2,1)S(1)} %copy-done, f32[5120]{0:T(1024)S(1)} %bitcast.184, f32[256]{0:T(256)S(1)} %add_rsqrt_fusion, ...), kind=kOutput, calls=%fused_computation.33 | convolution fusion | flops 1689026560 | bytes 12473601 | tf_op jit(solution)/shard_map/dot_general | solution.py:19
  237.0 0.0 reduce-scatter.5.cloned.1.call-update
  237.0 0.0 all-reduce.4.cloned.1.call-start
  237.1 10.2 %conditional.7 = (f32[256,5120]{1,0:T(8,128)}) conditional(s32[]{:T(128)} %convert_element_type.199, (bf16[256,640]{1,0:T(8,128)(2,1)S(1)}, bf16[5120,640]{1,0:T(8,128)(2,1)}) %tuple.78, (bf16[256,640]{1,0:T(8,128)(2,1)S(1)}, bf16[5120,640]{1,0:T(8,128)(2,1)}, pred[]{:T(512)}, bf16[1,256,640]{2,1,0:T(8,128)(2,1)S(1)}, ...), branch_computations={%region_11.12_spmd, %region_12.13_spmd} | conditional | flops 3356917760 | bytes 55705636 | solution.py:177
  237.3 5.3 fusion.59
  242.7 4.6 convolution_add_fusion
  247.3 0.0 all-reduce.4.cloned.1.call-update
  247.3 0.6 copy-done.12
  248.0 0.6 dynamic-slice
  249.2 55.4 %reduce-scatter.3.cloned.1.call-done = bf16[320,640]{1,0:T(8,128)(2,1)} async-done(((bf16[5120,640]{1,0:T(8,128)(2,1)}), bf16[320,640]{1,0:T(8,128)(2,1)}) %reduce-scatter.3.cloned.1.call-update) | async-done | bytes 409616 | tf_op jit(solution)/shard_map/reduce_scatter | solution.py:188
  304.6 1.9 bitcast_convert_fusion.1
  306.6 92.4 %reduce-scatter.5.cloned.1.call-done = bf16[320,640]{1,0:T(8,128)(2,1)} async-done(((bf16[5120,640]{1,0:T(8,128)(2,1)}), bf16[320,640]{1,0:T(8,128)(2,1)}) %reduce-scatter.5.cloned.1.call-update) | async-done | bytes 409616 | tf_op jit(solution)/shard_map/reduce_scatter | solution.py:191
  398.9 1.9 bitcast_convert_fusion
  400.9 194.1 %all-reduce.4.cloned.1.call-done = (f32[256,5120]{1,0:T(8,128)}, f32[256,5120]{1,0:T(8,128)}) async-done(((f32[256,5120]{1,0:T(8,128)}, f32[256,5120]{1,0:T(8,128)}), (f32[256,5120]{1,0:T(8,128)}, f32[256,5120]{1,0:T(8,128)})) %all-reduce.4.cloned.1.call-update) | async-done | bytes 10485776 | tf_op jit(solution)/shard_map/psum | solution.py:31
  595.0 5.3 fusion.40
  600.3 0.0 copy-done.4
  600.3 2.2 fusion.34
  602.5 3.8 fusion.41
  606.4 69.4 %all-reduce = bf16[5120]{0:T(1024)(128)(2,1)S(1)} all-reduce(bf16[5120]{0:T(1024)(128)(2,1)S(1)} %get-tuple-element.131), channel_id=4, replica_groups=mesh['section'=2,'dp'=16,'mp'=4] {'dp'}, use_global_device_ids=true, to_apply=%region_16.17.clone | all-reduce | flops 5120 | bytes 20480
  675.7 0.1 dynamic-slice_convert_fusion
  675.8 0.6 reshape.361
  (14 shorter events, 0.1 us)
Async XLA Ops:
  7.2 5.8 copy-start
  7.2 70.9 %copy-start.10 = (f32[1,5120]{1,0:T(1,128)S(1)}, f32[1,5120]{1,0:T(1,128)}, u32[]{:S(2)}) copy-start(f32[1,5120]{1,0:T(1,128)} %param.15) | copy-start | bytes 61444
  7.2 70.9 %all-gather.5.cloned.1.call-start = ((), (), s32[]{:S(2)}) async-start(), calls=%async_computation.4 | async-start | bytes 6963200 | tf_op jit(solution)/shard_map/all_gather | solution.py:99
  7.9 137.5 %all-gather.7.cloned.1.call-start = ((), (), s32[]{:S(2)}) async-start(), calls=%async_computation.5 | async-start | bytes 6963200 | tf_op jit(solution)/shard_map/all_gather | solution.py:100
  8.7 296.0 %reduce-scatter.3.cloned.1.call-start = ((), (), s32[]{:S(2)}) async-start(), calls=%async_computation.2 | async-start | bytes 6963200 | tf_op jit(solution)/shard_map/reduce_scatter | solution.py:188
  83.2 78.3 %copy-start.9 = (bf16[256,640]{1,0:T(8,128)(2,1)}, bf16[256,640]{1,0:T(8,128)(2,1)S(1)}, u32[]{:S(2)}) copy-start(bf16[256,640]{1,0:T(8,128)(2,1)S(1)} %convolution_convert_fusion.8) | copy-start | bytes 983044
  83.2 74.5 %collective-permute-start = (bf16[1,256,640]{2,1,0:T(8,128)(2,1)S(1)}, bf16[1,256,640]{2,1,0:T(8,128)(2,1)}, u32[]{:S(2)}, u32[]{:S(2)}) collective-permute-start(bf16[1,256,640]{2,1,0:T(8,128)(2,1)S(1)} %bitcast.180), channel_id=1, source_target_pairs={{0,64},{1,65},{2,66},{3,67},{4,68},{5,69},{6,70},{7,71},{8,72},{9,... | collective-permute-start | bytes 983048 | tf_op jit(solution)/shard_map/ppermute | solution.py:15
  151.3 10.2 %copy-start.11 = (s32[1,2]{1,0:T(1,128)S(1)}, s32[1,2]{1,0:T(1,128)}, u32[]{:S(2)}) copy-start(s32[1,2]{1,0:T(1,128)} %param.18) | copy-start | bytes 28
  152.2 9.3 %collective-permute-start.1 = (bf16[1,256,640]{1,2,0:T(8,128)(2,1)}, bf16[1,256,640]{1,2,0:T(8,128)(2,1)}, u32[]{:S(2)}, u32[]{:S(2)}) collective-permute-start(bf16[1,256,640]{1,2,0:T(8,128)(2,1)} %copy.53), channel_id=1, source_target_pairs={{0,64},{1,65},{2,66},{3,67},{4,68},{5,69},{6,70},{7,71},{8,72},{9,... | collective-permute-start | bytes 983048 | tf_op jit(solution)/shard_map/ppermute | solution.py:15
  169.1 42.2 %collective-permute-start.2 = (bf16[1,256,640]{2,1,0:T(8,128)(2,1)S(1)}, bf16[1,256,640]{2,1,0:T(8,128)(2,1)S(1)}, u32[]{:S(2)}, u32[]{:S(2)}) collective-permute-start(bf16[1,256,640]{2,1,0:T(8,128)(2,1)S(1)} %copy.59), channel_id=1, source_target_pairs={{64,0},{65,1},{66,2},{67,3},{68,4},{69,5},{70,6},{71,7},{72,8},{73... | collective-permute-start | bytes 983048 | tf_op jit(solution)/shard_map/ppermute | solution.py:15
  216.4 1.0 copy-start.8
  216.5 182.5 %reduce-scatter.5.cloned.1.call-start = ((), (), s32[]{:S(2)}) async-start(), calls=%async_computation.3 | async-start | bytes 6963200 | tf_op jit(solution)/shard_map/reduce_scatter | solution.py:191
  218.3 10.9 %collective-permute-start.3 = (bf16[1,256,640]{2,1,0:T(8,128)(2,1)}, bf16[1,256,640]{2,1,0:T(8,128)(2,1)S(1)}, u32[]{:S(2)}, u32[]{:S(2)}) collective-permute-start(bf16[1,256,640]{2,1,0:T(8,128)(2,1)} %copy.61), channel_id=1, source_target_pairs={{64,0},{65,1},{66,2},{67,3},{68,4},{69,5},{70,6},{71,7},{72,8},{73... | collective-permute-start | bytes 983048 | tf_op jit(solution)/shard_map/ppermute | solution.py:15
  237.0 358.0 %all-reduce.4.cloned.1.call-start = ((), (), s32[]{:S(2)}) async-start(), calls=%async_computation.6 | async-start | bytes 20971520 | tf_op jit(solution)/shard_map/psum | solution.py:31
  237.3 5.4 copy-start.2
  247.3 0.7 copy-start.12
  595.0 5.3 copy-start.3
  595.0 5.3 copy-start.4
Sparse Core Ops, SparseCore 0:
  10.5 67.5 all-gather.4
  80.5 64.8 all-gather.6
  216.6 88.0 reduce-scatter.2
  309.3 89.6 reduce-scatter.4
  401.4 193.5 all-reduce.3
where the time goes:
time: 684 us; the launch traced here: 683 us
  waiting for transfers between devices  519 us (76%)
  blocking collectives  69.4 us (10%)
  matrix products  33.8 us (5%)
  other arithmetic  24.8 us (4%)
  between operations  14.5 us (2%)
  local copies, waits for them, and re-layouts  13.3 us (2%)
  starting transfers between devices  8.01 us (1%)
    psum x1, waiting for transfers between devices, total_features(): return lax.psum(partial_value, 'mp')  194 us
    reduce_scatter x1, waiting for transfers between devices, shards(): lax.psum_scatter(weight_second.astype(jnp.bfloat16), 'dp', scatter_dimens...  92.4 us
    unnamed x1, blocking collectives  69.4 us
    all_gather x1, waiting for transfers between devices, shards(): lax.all_gather(w_first[0], 'dp', axis=0, tiled=True)  62.1 us
    all_gather x1, waiting for transfers between devices, shards(): lax.all_gather(w_second[0], 'dp', axis=0, tiled=True)  59 us
    reduce_scatter x1, waiting for transfers between devices, shards(): lax.psum_scatter(weight_first.astype(jnp.bfloat16), 'dp', scatter_dimensi...  55.4 us
    ppermute x4, waiting for transfers between devices, passed_along(): return lax.ppermute(shard, axis, pairs)  54.3 us
  transfers between devices with their start and end apart: 9, of which 8 were waited for; matrix products, arithmetic and copies ran while one was open for 7% of the time, Pallas kernels for 0%

commit v1 on v0

--- a/solution.py
+++ b/solution.py
@@ -28,7 +28,7 @@
 
 
 def total_features(partial_value):
-    return lax.psum(partial_value, "mp")
+    return jnp.sum(lax.all_gather(partial_value, "mp"), axis=0)
 
 
 def split_heads(values_in):

time: 684 us -> 886 us (1.30)
  waiting for transfers between devices: 519 us -> 697 us
  other arithmetic: 24.8 us -> 47.9 us
    all_gather x0 -> x2, waiting for transfers between devices: none -> 362 us  [total_features(): return jnp.sum(lax.all_gather(partial_value, 'mp'), axis=0)]
    psum x1 -> x0, waiting for transfers between devices: 194 us -> none  [total_features(): return lax.psum(partial_value, 'mp')]
    reduce_scatter x1, waiting for transfers between devices: 55.4 us -> 92.4 us  [shards(): lax.psum_scatter(weight_first.astype(jnp.bfloat16), 'dp', scatter_dimensi...]
    reduce_scatter x1, waiting for transfers between devices: 92.4 us -> 59.7 us  [shards(): lax.psum_scatter(weight_second.astype(jnp.bfloat16), 'dp', scatter_dimens...]
    reduce_sum x0 -> x2, other arithmetic: none -> 22.3 us  [total_features(): return jnp.sum(lax.all_gather(partial_value, 'mp'), axis=0)]
  transfers between devices with their start and end apart: 9 -> 10, of which waited for: 8 -> 9; matrix products, arithmetic and copies ran while one was open for 7% -> 7% of each run, Pallas kernels for 0% -> 0%
where the time goes in v1:
time: 886 us; the launch traced here: 885 us
  waiting for transfers between devices  697 us (79%)
  blocking collectives  69.4 us (8%)
  other arithmetic  47.9 us (5%)
  matrix products  34.8 us (4%)
  between operations  14.9 us (2%)
  local copies, waits for them, and re-layouts  13.1 us (1%)
    all_gather x2, waiting for transfers between devices, total_features(): return jnp.sum(lax.all_gather(partial_value, 'mp'), axis=0)  362 us
    reduce_scatter x1, waiting for transfers between devices, shards(): lax.psum_scatter(weight_first.astype(jnp.bfloat16), 'dp', scatter_dimensi...  92.4 us
    unnamed x1, blocking collectives  69.4 us
    all_gather x1, waiting for transfers between devices, shards(): lax.all_gather(w_second[0], 'dp', axis=0, tiled=True)  64 us
    reduce_scatter x1, waiting for transfers between devices, shards(): lax.psum_scatter(weight_second.astype(jnp.bfloat16), 'dp', scatter_dimens...  59.7 us
    all_gather x1, waiting for transfers between devices, shards(): lax.all_gather(w_first[0], 'dp', axis=0, tiled=True)  59.1 us
    ppermute x4, waiting for transfers between devices, passed_along(): return lax.ppermute(shard, axis, pairs)  57.1 us
    reduce_sum x2, other arithmetic, total_features(): return jnp.sum(lax.all_gather(partial_value, 'mp'), axis=0)  22.3 us
  transfers between devices with their start and end apart: 10, of which 9 were waited for; matrix products, arithmetic and copies ran while one was open for 7% of the time, Pallas kernels for 0%

profile of v1, /device:TPU:0, one launch (start us, length us, event | category | flops | bytes accessed | tf_op | source)
XLA Modules:
  0.0 884.7 jit_solution(15287927350816567501)
XLA Ops:
  7.2 0.0 all-gather.11.cloned.1.call-start
  7.2 0.7 all-gather.11.cloned.1.call-update
  7.9 0.0 all-gather.9.cloned.1.call-start
  8.0 0.7 all-gather.9.cloned.1.call-update
  8.7 0.0 reduce-scatter.5.cloned.1.call-start
  8.7 2.3 fusion.37
  11.1 3.0 fusion.43
  14.1 64.0 %all-gather.11.cloned.1.call-done = bf16[1,5120,640]{2,1,0:T(8,128)(2,1)} async-done(((bf16[1,320,640]{2,1,0:T(8,128)(2,1)}), bf16[1,5120,640]{2,1,0:T(8,128)(2,1)}) %all-gather.11.cloned.1.call-update) | async-done | bytes 6553616 | tf_op jit(solution)/shard_map/all_gather | solution.py:100
  78.1 5.9 conditional.4
  78.1 5.9 fusion
  83.9 0.9 copy.53
  84.8 2.2 collective-permute-start.1
  87.0 59.1 %all-gather.9.cloned.1.call-done = bf16[1,5120,640]{2,1,0:T(8,128)(2,1)} async-done(((bf16[1,320,640]{2,1,0:T(8,128)(2,1)}), bf16[1,5120,640]{2,1,0:T(8,128)(2,1)}) %all-gather.9.cloned.1.call-update) | async-done | bytes 6553616 | tf_op jit(solution)/shard_map/all_gather | solution.py:99
  146.1 5.9 convolution_convert_fusion.7
  151.9 3.2 collective-permute-start
  155.2 0.6 slice.6
  155.7 0.6 iota_compare_fusion.1
  156.4 0.0 collective-permute-done.1
  156.4 5.4 collective-permute-done
  161.8 5.8 conditional.5
  161.8 3.0 broadcast.183
  164.8 1.2 broadcast.181
  166.0 0.9 broadcast.182
  166.9 0.8 broadcast.180.clone
  167.6 1.5 conditional.6
  167.6 0.7 broadcast.185
  168.4 0.8 broadcast.185.clone
  169.2 0.2 copy.61
  169.4 1.3 collective-permute-start.3
  170.7 42.7 %collective-permute-done.3 = bf16[1,256,640]{2,1,0:T(8,128)(2,1)S(1)} collective-permute-done((bf16[1,256,640]{2,1,0:T(8,128)(2,1)S(1)}, bf16[1,256,640]{2,1,0:T(8,128)(2,1)S(1)}, u32[]{:S(2)}, u32[]{:S(2)}) %collective-permute-start.3) | collective-permute-done | bytes 327712 | tf_op jit(solution)/shard_map/ppermute | solution.py:15
  213.4 0.7 copy-done.8
  214.1 7.6 convolution_convert_fusion.5
  221.7 0.0 reduce-scatter.5.cloned.1.call-update
  221.7 0.0 reduce-scatter.3.cloned.1.call-start
  221.8 1.2 copy.59
  223.0 1.3 collective-permute-start.2
  224.3 9.0 %collective-permute-done.2 = bf16[1,256,640]{2,1,0:T(8,128)(2,1)S(1)} collective-permute-done((bf16[1,256,640]{2,1,0:T(8,128)(2,1)S(1)}, bf16[1,256,640]{2,1,0:T(8,128)(2,1)S(1)}, u32[]{:S(2)}, u32[]{:S(2)}) %collective-permute-start.2) | collective-permute-done | bytes 327712 | tf_op jit(solution)/shard_map/ppermute | solution.py:15
  233.3 5.2 convolution_convert_fusion.6
  238.5 0.0 reduce-scatter.3.cloned.1.call-update
  238.6 0.0 all-gather.13.cloned.1.call-start
  238.6 0.5 all-gather.13.cloned.1.call-update
  239.2 0.0 all-gather.15.cloned.1.call-start
  239.2 0.3 copy-done.9
  239.5 10.3 %conditional.7 = (f32[256,5120]{1,0:T(8,128)}) conditional(s32[]{:T(128)} %convert_element_type.211, (bf16[256,640]{1,0:T(8,128)(2,1)S(1)}, bf16[5120,640]{1,0:T(8,128)(2,1)}) %tuple.79, (bf16[256,640]{1,0:T(8,128)(2,1)S(1)}, bf16[5120,640]{1,0:T(8,128)(2,1)}, pred[]{:T(512)}, bf16[1,256,640]{2,1,0:T(8,128)(2,1)S(1)}, ...), branch_computations={%region_11.12_spmd, %region_12.13_spmd} | conditional | flops 3356917760 | bytes 55705636 | solution.py:177
  239.5 5.7 fusion.64
  245.3 4.5 convolution_add_fusion
  249.8 0.0 all-gather.15.cloned.1.call-update
  249.8 0.6 copy-done.11
  250.5 0.6 dynamic-slice
  251.7 59.7 %reduce-scatter.5.cloned.1.call-done = bf16[320,640]{1,0:T(8,128)(2,1)} async-done(((bf16[5120,640]{1,0:T(8,128)(2,1)}), bf16[320,640]{1,0:T(8,128)(2,1)}) %reduce-scatter.5.cloned.1.call-update) | async-done | bytes 409616 | tf_op jit(solution)/shard_map/reduce_scatter | solution.py:191
  311.4 1.9 bitcast_convert_fusion
  313.3 92.4 %reduce-scatter.3.cloned.1.call-done = bf16[320,640]{1,0:T(8,128)(2,1)} async-done(((bf16[5120,640]{1,0:T(8,128)(2,1)}), bf16[320,640]{1,0:T(8,128)(2,1)}) %reduce-scatter.3.cloned.1.call-update) | async-done | bytes 409616 | tf_op jit(solution)/shard_map/reduce_scatter | solution.py:188
  405.7 1.9 bitcast_convert_fusion.1
  407.6 188.3 %all-gather.13.cloned.1.call-done = f32[1024,5120]{1,0:T(8,128)} async-done(((f32[256,5120]{1,0:T(8,128)}), f32[1024,5120]{1,0:T(8,128)}) %all-gather.13.cloned.1.call-update) | async-done | bytes 20971536 | tf_op jit(solution)/shard_map/all_gather | solution.py:31
  595.9 11.2 %reduce_sum.68 = f32[256,5120]{1,0:T(8,128)} reduce(f32[4,256,5120]{2,1,0:T(8,128)} %bitcast.148, f32[]{:T(128)} %constant.23.clone.1), dimensions={0}, to_apply=%region_7.8 | reduce | flops 3932160 | bytes 26214404 | tf_op jit(solution)/shard_map/reduce_sum | solution.py:31
  607.1 6.2 fusion.47
  613.3 174.0 %all-gather.15.cloned.1.call-done = f32[1024,5120]{1,0:T(8,128)} async-done(((f32[256,5120]{1,0:T(8,128)}), f32[1024,5120]{1,0:T(8,128)}) %all-gather.15.cloned.1.call-update) | async-done | bytes 20971536 | tf_op jit(solution)/shard_map/all_gather | solution.py:31
  787.4 11.1 %reduce_sum.70 = f32[256,5120]{1,0:T(8,128)} reduce(f32[4,256,5120]{2,1,0:T(8,128)} %bitcast.149, f32[]{:T(128)} %constant.23.clone.1), dimensions={0}, to_apply=%region_13.14 | reduce | flops 3932160 | bytes 26214404 | tf_op jit(solution)/shard_map/reduce_sum | solution.py:31
  798.4 5.5 fusion.45
  804.0 0.0 copy-done.3
  804.0 3.8 fusion.36
  807.9 69.4 %all-reduce = bf16[5120]{0:T(1024)(128)(2,1)S(1)} all-reduce(bf16[5120]{0:T(1024)(128)(2,1)S(1)} %get-tuple-element.141), channel_id=6, replica_groups=mesh['section'=2,'dp'=16,'mp'=4] {'dp'}, use_global_device_ids=true, to_apply=%region_16.17.clone | all-reduce | flops 5120 | bytes 20480
  877.2 0.1 dynamic-slice_convert_fusion
  877.3 0.6 reshape.411
  (20 shorter events, 0.1 us)
Async XLA Ops:
  7.2 3.9 copy-start
  7.2 70.9 %all-gather.11.cloned.1.call-start = ((), (), s32[]{:S(2)}) async-start(), calls=%async_computation.5 | async-start | bytes 6963200 | tf_op jit(solution)/shard_map/all_gather | solution.py:100
  7.9 138.2 %all-gather.9.cloned.1.call-start = ((), (), s32[]{:S(2)}) async-start(), calls=%async_computation.4 | async-start | bytes 6963200 | tf_op jit(solution)/shard_map/all_gather | solution.py:99
  8.7 302.7 %reduce-scatter.5.cloned.1.call-start = ((), (), s32[]{:S(2)}) async-start(), calls=%async_computation.3 | async-start | bytes 6963200 | tf_op jit(solution)/shard_map/reduce_scatter | solution.py:191
  84.8 70.3 %copy-start.10 = (s32[1,2]{1,0:T(1,128)S(1)}, s32[1,2]{1,0:T(1,128)}, u32[]{:S(2)}) copy-start(s32[1,2]{1,0:T(1,128)} %param.18) | copy-start | bytes 28
  84.8 71.6 %collective-permute-start.1 = (bf16[1,256,640]{1,2,0:T(8,128)(2,1)}, bf16[1,256,640]{1,2,0:T(8,128)(2,1)}, u32[]{:S(2)}, u32[]{:S(2)}) collective-permute-start(bf16[1,256,640]{1,2,0:T(8,128)(2,1)} %copy.53), channel_id=1, source_target_pairs={{0,64},{1,65},{2,66},{3,67},{4,68},{5,69},{6,70},{7,71},{8,72},{9,... | collective-permute-start | bytes 983048 | tf_op jit(solution)/shard_map/ppermute | solution.py:15
  151.9 9.9 %collective-permute-start = (bf16[1,256,640]{2,1,0:T(8,128)(2,1)S(1)}, bf16[1,256,640]{2,1,0:T(8,128)(2,1)}, u32[]{:S(2)}, u32[]{:S(2)}) collective-permute-start(bf16[1,256,640]{2,1,0:T(8,128)(2,1)S(1)} %bitcast.159), channel_id=1, source_target_pairs={{0,64},{1,65},{2,66},{3,67},{4,68},{5,69},{6,70},{7,71},{8,72},{9,... | collective-permute-start | bytes 983048 | tf_op jit(solution)/shard_map/ppermute | solution.py:15
  167.6 46.5 %copy-start.7 = (f32[1,5120]{1,0:T(1,128)S(1)}, f32[1,5120]{1,0:T(1,128)}, u32[]{:S(2)}) copy-start(f32[1,5120]{1,0:T(1,128)} %param.15) | copy-start | bytes 61444
  169.4 44.0 %collective-permute-start.3 = (bf16[1,256,640]{2,1,0:T(8,128)(2,1)S(1)}, bf16[1,256,640]{2,1,0:T(8,128)(2,1)S(1)}, u32[]{:S(2)}, u32[]{:S(2)}) collective-permute-start(bf16[1,256,640]{2,1,0:T(8,128)(2,1)S(1)} %copy.61), channel_id=1, source_target_pairs={{64,0},{65,1},{66,2},{67,3},{68,4},{69,5},{70,6},{71,7},{72,8},{73... | collective-permute-start | bytes 983048 | tf_op jit(solution)/shard_map/ppermute | solution.py:15
  213.4 0.7 copy-start.8
  221.7 11.6 %copy-start.5 = (bf16[1,256,640]{2,1,0:T(8,128)(2,1)S(1)}, bf16[1,256,640]{2,1,0:T(8,128)(2,1)}, u32[]{:S(2)}) copy-start(bf16[1,256,640]{2,1,0:T(8,128)(2,1)} %get-tuple-element.140) | copy-start | bytes 983044
  221.7 184.0 %reduce-scatter.3.cloned.1.call-start = ((), (), s32[]{:S(2)}) async-start(), calls=%async_computation.2 | async-start | bytes 6963200 | tf_op jit(solution)/shard_map/reduce_scatter | solution.py:188
  223.0 10.3 %collective-permute-start.2 = (bf16[1,256,640]{2,1,0:T(8,128)(2,1)S(1)}, bf16[1,256,640]{2,1,0:T(8,128)(2,1)S(1)}, u32[]{:S(2)}, u32[]{:S(2)}) collective-permute-start(bf16[1,256,640]{2,1,0:T(8,128)(2,1)S(1)} %copy.59), channel_id=1, source_target_pairs={{64,0},{65,1},{66,2},{67,3},{68,4},{69,5},{70,6},{71,7},{72,8},{73... | collective-permute-start | bytes 983048 | tf_op jit(solution)/shard_map/ppermute | solution.py:15
  238.5 1.0 copy-start.9
  238.6 357.3 %all-gather.13.cloned.1.call-start = ((), (), s32[]{:S(2)}) async-start(), calls=%async_computation.6 | async-start | bytes 26214400 | tf_op jit(solution)/shard_map/all_gather | solution.py:31
  239.2 548.2 %all-gather.15.cloned.1.call-start = ((), (), s32[]{:S(2)}) async-start(), calls=%async_computation.7 | async-start | bytes 26214400 | tf_op jit(solution)/shard_map/all_gather | solution.py:31
  239.5 5.7 copy-start.2
  249.8 0.7 copy-start.11
  798.4 5.6 copy-start.1
  798.4 5.6 copy-start.3
Sparse Core Ops, SparseCore 0:
  10.5 67.5 all-gather.10
  80.5 65.5 all-gather.8
  221.8 89.5 reduce-scatter.4
  316.0 89.6 reduce-scatter.2
  407.2 188.6 all-gather.12
  597.4 189.9 all-gather.14
